TPU v7x, 128 devices: a whole 4x4x4 slice. The times are simulated.
128 devices in a mesh: fsdp: 4 (over y_lo, core), ctx: 8 (over y_hi, z), tp: 4 (over x).
Axes of the slice: x: 4, y: 4 (y_hi: 2, y_lo: 2; y = y_hi * 2 + y_lo), z: 4, core: 2. Of those that a mesh axis runs over, the one named last changes fastest.
Arguments:
- layer_input: bfloat16 [16, 2048, 768], P('fsdp', 'ctx'), may hold values from -6 to 6
- segment_ids: int32 [16, 2048], P('fsdp', 'ctx'), may hold values from 0 to 3, never falling along the last dimension, each value on 1 to 1280 neighbouring positions
- proj_weight: bfloat16 [3, 768, 768], P(None, 'fsdp', 'tp'), may hold values from -0.21875 to 0.21875
- proj_bias: bfloat16 [2, 768], P(None, 'tp'), may hold values from -3 to 3
- out_weight: bfloat16 [768, 768], P('tp', 'fsdp'), may hold values from -2.5 to 2.5
- out_bias: bfloat16 [768], P('fsdp'), may hold values from -3 to 3
- first_gain: bfloat16 [768], P('fsdp'), may hold values from 0.099609375 to 1.8984375
- first_shift: bfloat16 [768], P('fsdp'), may hold values from -2 to 2
- up_weight: bfloat16 [768, 3072], P('fsdp', 'tp'), may hold values from -0.21875 to 0.21875
- up_bias: bfloat16 [3072], P('tp'), may hold values from -3 to 3
- down_weight: bfloat16 [3072, 768], P('tp', 'fsdp'), may hold values from -0.15625 to 0.15625
- down_bias: bfloat16 [768], P('fsdp'), may hold values from -2 to 2
- second_gain: bfloat16 [768], P('fsdp'), may hold values from 0.099609375 to 1.8984375
- second_shift: bfloat16 [768], P('fsdp'), may hold values from -2 to 2
- cotangent: bfloat16 [16, 2048, 768], P('fsdp', 'ctx'), may hold values from -6 to 6
Outputs:
- layer_output: bfloat16 [16, 2048, 768], P('fsdp', 'ctx')
- input_grad: float32 [16, 2048, 768], P('fsdp', 'ctx')
- proj_grad: float32 [3, 768, 768], P(None, ('fsdp', 'ctx'), 'tp')
- proj_bias_grad: float32 [2, 768], P(None, 'tp')
- out_grad: float32 [768, 768], P('tp', ('fsdp', 'ctx'))
- out_bias_grad: float32 [768], P(('fsdp', 'ctx'))
- first_gain_grad: float32 [768], P(('fsdp', 'ctx'))
- first_shift_grad: float32 [768], P(('fsdp', 'ctx'))
- up_grad: float32 [768, 3072], P(('fsdp', 'ctx'), 'tp')
- up_bias_grad: float32 [3072], P('tp')
- down_grad: float32 [3072, 768], P('tp', ('fsdp', 'ctx'))
- down_bias_grad: float32 [768], P(('fsdp', 'ctx'))
- second_gain_grad: float32 [768], P(('fsdp', 'ctx'))
- second_shift_grad: float32 [768], P(('fsdp', 'ctx'))
Inputs may be any that keep to these rules, and one draw needn't show every extreme that they name: `segment_ids`: ids never fall along a sequence; every document spans 1 to 1280 positions, and one in each sequence spans exactly 1280.
All inputs are finite; a program needn't handle non-finite values.
Results may differ from a plain program's by a relative error of at most 0.039.
Values may be sent and summed in bfloat16 or wider, within the bound.
A program may use at most 192 MiB of HBM per device.

v0:
```python
import jax
import jax.numpy as jnp
from jax import lax
from jax.sharding import PartitionSpec as P

HEAD_DIM = 64
norm_eps = 1e-12
masked_score = -1e30


def turned_gather(arrays, axis, dims):
    turned = [jnp.moveaxis(a, dim, 0) for a, dim in zip(arrays, dims)]
    widths = [t[0].size for t in turned]
    both = jnp.concatenate([t.reshape(-1, w) for t, w in zip(turned, widths)], axis=1)
    out = lax.all_gather(both, axis, axis=0, tiled=True)
    pieces = jnp.split(out, [sum(widths[:k]) for k in range(1, len(widths))], axis=1)
    return tuple(
        (
            jnp.moveaxis(b.reshape(-1, *t.shape[1:]), 0, dim)
            for b, t, dim in zip(pieces, turned, dims)
        )
    )


def sent_together(arrays, axis, dim, along):
    ends, at = ([], 0)
    for a in arrays[:-1]:
        at += a.shape[along]
        ends.append(at)
    both = jnp.concatenate(arrays, axis=along)
    return tuple(jnp.split(lax.all_gather(both, axis, axis=dim, tiled=True), ends, axis=along))


def rows_for(lines, count):
    spare = -len(lines) % count
    return jnp.pad(lines, [(0, spare)] + [(0, 0)] * (lines.ndim - 1))


def sum_by_parts(x, axis):
    lines = x.reshape(-1, *x.shape[1:][-1:])
    padded = rows_for(lines, lax.axis_size(axis))
    own = lax.psum_scatter(padded, axis, scatter_dimension=0, tiled=True)
    whole = lax.all_gather(own, axis, axis=0, tiled=True)
    return whole[: len(lines)].reshape(x.shape)


def cut_along(x, dim, count):
    shape = x.shape
    pieces = x.reshape(*shape[:dim], count, shape[dim] // count, *shape[dim + 1 :])
    return jnp.moveaxis(pieces, dim, 0)


def sum_together(arrays, axis, dims):
    count = lax.axis_size(axis)
    pieces = [cut_along(a, dim, count) for a, dim in zip(arrays, dims)]
    lines = jnp.concatenate([b.reshape(count, -1) for b in pieces], axis=1)
    width = max(16, -(-lines.shape[1] // 1024) * 8)
    lines = jnp.pad(lines, ((0, 0), (0, width * 128 - lines.shape[1]))).reshape(-1, 128)
    flat, at, outs = (lax.psum_scatter(lines, axis, tiled=True).reshape(-1), 0, [])
    for b in pieces:
        part = b[0]
        outs.append(flat[at : at + part.size].reshape(part.shape))
        at += part.size
    return tuple(outs)


def sent_to_all(x, axis):
    count = lax.axis_size(axis)
    return lax.all_to_all(jnp.broadcast_to(x[None], (count, *x.shape)), axis, 0, 0, tiled=True)


def of_everyone(x, axis):
    return sent_to_all(x, axis).sum(axis=0)


def packed_total(arrays, axis):
    ends = [0]
    for a in arrays:
        ends.append(ends[-1] + a.size)
    subtotal = of_everyone(jnp.concatenate([a.ravel() for a in arrays]), axis)
    return tuple((subtotal[b:e].reshape(a.shape) for a, b, e in zip(arrays, ends, ends[1:])))


def layer_norm(values_in, gain, shift):
    centre = jnp.mean(values_in, axis=-1, keepdims=True)
    centred = values_in - centre
    spread = jnp.mean(centred * centred, axis=-1, keepdims=True)
    return centred * lax.rsqrt(spread + norm_eps) * gain + shift


def gelu_exact(values_in):
    return jax.nn.gelu(values_in, approximate=False)


def doc_scores(queries, key_rows, query_docs, key_docs):
    raw_scores = jnp.einsum(
        "sqhd,skhd->shqk", queries, key_rows, preferred_element_type=jnp.float32
    ) * HEAD_DIM ** (-0.5)
    same_doc = query_docs[:, None, :, None] == key_docs[:, None, None, :]
    return (raw_scores, same_doc)


def whole_attention(queries, key_rows, value_rows, query_docs, key_docs):
    raw_scores, same_doc = doc_scores(queries, key_rows, query_docs, key_docs)
    row_high = jnp.max(jnp.where(same_doc, raw_scores, masked_score), axis=-1, keepdims=True)
    exp_terms = jnp.where(same_doc, jnp.exp(raw_scores - row_high), 0.0)
    row_total = jnp.sum(exp_terms, axis=-1, keepdims=True)
    attn_probs = (exp_terms / row_total).astype(jnp.bfloat16)
    attended = jnp.einsum(
        "shqk,skhd->sqhd", attn_probs, value_rows, preferred_element_type=jnp.float32
    )
    return (attended, row_high + jnp.log(row_total))


def queries_back(queries, key_rows, value_rows, query_docs, key_docs, log_total, grad_context):
    raw_scores, same_doc = doc_scores(queries, key_rows, query_docs, key_docs)
    attn_probs = jnp.where(same_doc, jnp.exp(raw_scores - log_total), 0.0)
    grad_probs = jnp.einsum(
        "sqhd,skhd->shqk", grad_context, value_rows, preferred_element_type=jnp.float32
    )
    row_delta = jnp.sum(attn_probs * grad_probs, axis=-1, keepdims=True)
    grad_scores = (attn_probs * (grad_probs - row_delta)).astype(jnp.bfloat16)
    grad_queries = jnp.einsum(
        "shqk,skhd->sqhd", grad_scores, key_rows, preferred_element_type=jnp.float32
    ) * HEAD_DIM ** (-0.5)
    return (grad_queries, row_delta)


def keys_back(
    all_queries,
    own_keys,
    own_values,
    all_query_docs,
    own_docs,
    all_log_total,
    all_delta,
    all_grad_context,
):
    raw_scores, same_doc = doc_scores(all_queries, own_keys, all_query_docs, own_docs)
    attn_probs = jnp.where(same_doc, jnp.exp(raw_scores - all_log_total), 0.0)
    probs_low = attn_probs.astype(jnp.bfloat16)
    grad_probs = jnp.einsum(
        "sqhd,skhd->shqk", all_grad_context, own_values, preferred_element_type=jnp.float32
    )
    grad_scores = (attn_probs * (grad_probs - all_delta)).astype(jnp.bfloat16)
    grad_keys = jnp.einsum(
        "shqk,sqhd->skhd", grad_scores, all_queries, preferred_element_type=jnp.float32
    ) * HEAD_DIM ** (-0.5)
    grad_values = jnp.einsum(
        "shqk,sqhd->skhd", probs_low, all_grad_context, preferred_element_type=jnp.float32
    )
    return (grad_keys, grad_values)


def shards(
    layer_input,
    segment_ids,
    proj_weight,
    proj_bias,
    out_weight,
    out_bias,
    first_gain,
    first_shift,
    up_weight,
    up_bias,
    down_weight,
    down_bias,
    second_gain,
    second_shift,
    cotangent,
):
    seq_count, group_len, model_width = layer_input.shape
    local_cols = proj_weight.shape[2]
    head_count = local_cols // HEAD_DIM
    row_count = seq_count * group_len
    (
        proj_full,
        out_full,
        up_full,
        down_full,
        out_shift,
        down_shift,
        gain_one,
        shift_one,
        gain_two,
        shift_two,
    ) = turned_gather(
        (
            proj_weight,
            out_weight,
            up_weight,
            down_weight,
            out_bias,
            down_bias,
            first_gain,
            first_shift,
            second_gain,
            second_shift,
        ),
        "fsdp",
        (1, 1, 0, 1, 0, 0, 0, 0, 0, 0),
    )
    gain_one = gain_one.astype(jnp.float32)
    shift_one = shift_one.astype(jnp.float32)
    gain_two = gain_two.astype(jnp.float32)
    shift_two = shift_two.astype(jnp.float32)
    flat_rows = layer_input.reshape(row_count, model_width)
    bias_pair = proj_bias.astype(jnp.float32)
    proj_pre = jnp.einsum("rd,tdc->trc", flat_rows, proj_full, preferred_element_type=jnp.float32)
    head_shape = (seq_count, group_len, head_count, HEAD_DIM)
    queries = (proj_pre[0] + bias_pair[0]).astype(jnp.bfloat16).reshape(head_shape)
    key_rows = proj_pre[1].astype(jnp.bfloat16).reshape(head_shape)
    value_rows = (proj_pre[2] + bias_pair[1]).astype(jnp.bfloat16).reshape(head_shape)
    all_keys, all_values, all_docs = (
        *sent_together((key_rows, value_rows), "ctx", 1, 0),
        lax.all_gather(segment_ids, "ctx", axis=1, tiled=True),
    )
    attended, log_total = whole_attention(queries, all_keys, all_values, segment_ids, all_docs)
    context = attended.reshape(row_count, local_cols).astype(jnp.bfloat16)
    attn_part = jnp.dot(context, out_full, preferred_element_type=jnp.float32)
    attn_full = lax.psum(attn_part.astype(jnp.bfloat16), "tp").astype(jnp.float32)
    first_sum = flat_rows.astype(jnp.float32) + attn_full + out_shift.astype(jnp.float32)
    first_norm = layer_norm(first_sum, gain_one, shift_one)
    norm_low = first_norm.astype(jnp.bfloat16)
    up_pre = jnp.dot(norm_low, up_full, preferred_element_type=jnp.float32) + up_bias.astype(
        jnp.float32
    )
    activated = gelu_exact(up_pre).astype(jnp.bfloat16)
    ffn_part = jnp.dot(activated, down_full, preferred_element_type=jnp.float32)
    ffn_full = lax.psum(ffn_part.astype(jnp.bfloat16), "tp").astype(jnp.float32)
    second_sum = first_norm + ffn_full + down_shift.astype(jnp.float32)
    second_norm, second_pull = jax.vjp(layer_norm, second_sum, gain_two, shift_two)
    layer_output = second_norm.astype(jnp.bfloat16).reshape(seq_count, group_len, model_width)
    grad_second, grad_gain_two, grad_shift_two = second_pull(
        cotangent.reshape(row_count, model_width).astype(jnp.float32)
    )
    grad_down_bias = jnp.sum(grad_second, axis=0)
    second_low = grad_second.astype(jnp.bfloat16)
    grad_down = jnp.einsum("rf,rd->fd", activated, second_low, preferred_element_type=jnp.float32)
    grad_active = jnp.einsum(
        "rd,fd->rf", second_low, down_full, preferred_element_type=jnp.float32
    ).astype(jnp.bfloat16)
    gelu_value, gelu_pull = jax.vjp(gelu_exact, up_pre)
    grad_up_pre = gelu_pull(grad_active.astype(jnp.float32))[0]
    grad_up_bias = jnp.sum(grad_up_pre, axis=0)
    up_low = grad_up_pre.astype(jnp.bfloat16)
    grad_up = jnp.einsum("rd,rf->df", norm_low, up_low, preferred_element_type=jnp.float32)
    norm_part = jnp.einsum("rf,df->rd", up_low, up_full, preferred_element_type=jnp.float32)
    grad_norm = grad_second + lax.psum(norm_part.astype(jnp.bfloat16), "tp").astype(jnp.float32)
    first_value, first_pull = jax.vjp(layer_norm, first_sum, gain_one, shift_one)
    grad_first, grad_gain_one, grad_shift_one = first_pull(grad_norm)
    grad_out_bias = jnp.sum(grad_first, axis=0)
    first_low = grad_first.astype(jnp.bfloat16)
    grad_out = jnp.einsum("rc,rd->cd", context, first_low, preferred_element_type=jnp.float32)
    grad_context = (
        jnp.einsum("rd,cd->rc", first_low, out_full, preferred_element_type=jnp.float32)
        .astype(jnp.bfloat16)
        .reshape(head_shape)
    )
    back_keys, back_values, back_docs = (all_keys, all_values, all_docs)
    grad_queries, row_delta = queries_back(
        queries, back_keys, back_values, segment_ids, back_docs, log_total, grad_context
    )
    all_queries, all_grad_context, all_query_docs = (
        *sent_together((queries, grad_context), "ctx", 1, 0),
        lax.all_gather(segment_ids, "ctx", axis=1, tiled=True),
    )
    all_log_total, all_delta = sent_together((log_total, row_delta), "ctx", 2, 0)
    grad_keys, grad_values = keys_back(
        all_queries,
        key_rows,
        value_rows,
        all_query_docs,
        segment_ids,
        all_log_total,
        all_delta,
        all_grad_context,
    )
    grad_query_flat = grad_queries.reshape(row_count, local_cols)
    grad_value_flat = grad_values.reshape(row_count, local_cols)
    grad_proj_bias = jnp.stack([jnp.sum(grad_query_flat, axis=0), jnp.sum(grad_value_flat, axis=0)])
    grad_stack = jnp.stack(
        [grad_query_flat, grad_keys.reshape(row_count, local_cols), grad_value_flat]
    ).astype(jnp.bfloat16)
    grad_proj = jnp.einsum("rd,trc->tdc", flat_rows, grad_stack, preferred_element_type=jnp.float32)
    input_part = jnp.einsum(
        "trc,tdc->rd", grad_stack, proj_full, preferred_element_type=jnp.float32
    )
    input_grad = (
        grad_first + sum_by_parts(input_part.astype(jnp.bfloat16), "tp").astype(jnp.float32)
    ).reshape(seq_count, group_len, model_width)
    (
        proj_grad,
        out_grad,
        up_grad,
        down_grad,
        out_bias_grad,
        down_bias_grad,
        first_gain_grad,
        first_shift_grad,
        second_gain_grad,
        second_shift_grad,
    ) = tuple(
        (
            part.astype(jnp.float32)
            for part in sum_together(
                (
                    grad_proj.astype(jnp.bfloat16),
                    grad_out.astype(jnp.bfloat16),
                    grad_up.astype(jnp.bfloat16),
                    grad_down.astype(jnp.bfloat16),
                    grad_out_bias.astype(jnp.bfloat16),
                    grad_down_bias.astype(jnp.bfloat16),
                    grad_gain_one.astype(jnp.bfloat16),
                    grad_shift_one.astype(jnp.bfloat16),
                    grad_gain_two.astype(jnp.bfloat16),
                    grad_shift_two.astype(jnp.bfloat16),
                ),
                ("fsdp", "ctx"),
                (1, 1, 0, 1, 0, 0, 0, 0, 0, 0),
            )
        )
    )
    proj_bias_grad, up_bias_grad = packed_total((grad_proj_bias, grad_up_bias), ("fsdp", "ctx"))
    return (
        layer_output,
        input_grad,
        proj_grad,
        proj_bias_grad,
        out_grad,
        out_bias_grad,
        first_gain_grad,
        first_shift_grad,
        up_grad,
        up_bias_grad,
        down_grad,
        down_bias_grad,
        second_gain_grad,
        second_shift_grad,
    )


def solution(mesh):
    placed = (
        P("fsdp", "ctx", None),
        P("fsdp", "ctx"),
        P(None, "fsdp", "tp"),
        P(None, "tp"),
        P("tp", "fsdp"),
        P("fsdp"),
        P("fsdp"),
        P("fsdp"),
        P("fsdp", "tp"),
        P("tp"),
        P("tp", "fsdp"),
        P("fsdp"),
        P("fsdp"),
        P("fsdp"),
        P("fsdp", "ctx", None),
    )
    return jax.shard_map(
        shards,
        mesh=mesh,
        in_specs=placed,
        out_specs=(
            P("fsdp", "ctx", None),
            P("fsdp", "ctx", None),
            P(None, ("fsdp", "ctx"), "tp"),
            P(None, "tp"),
            P("tp", ("fsdp", "ctx")),
            P(("fsdp", "ctx")),
            P(("fsdp", "ctx")),
            P(("fsdp", "ctx")),
            P(("fsdp", "ctx"), "tp"),
            P("tp"),
            P("tp", ("fsdp", "ctx")),
            P(("fsdp", "ctx")),
            P(("fsdp", "ctx")),
            P(("fsdp", "ctx")),
        ),
        check_vma=False,
    )
```

profile of v0, /device:TPU:1, one launch (start us, length us, event | category | flops | bytes accessed | tf_op | source)
XLA Modules:
  0.0 778.4 jit_solution(16677096041173922460)
XLA Ops:
  14.1 3.2 concatenate.18
  17.5 46.3 %all-gather.5.cloned.1.call-done = bf16[768,2310]{1,0:T(8,128)(2,1)} async-done(((bf16[192,2310]{1,0:T(8,128)(2,1)}), bf16[768,2310]{1,0:T(8,128)(2,1)}) %all-gather.5.cloned.1.call-update) | async-done | bytes 3548176 | tf_op jit(solution)/shard_map/all_gather | solution.py:15
  70.7 28.1 %all_gather.21 = s32[4,2048]{1,0:T(4,128)S(1)} all-gather(s32[4,256]{1,0:T(4,128)S(1)} %copy-done.34), channel_id=1, replica_groups=mesh['fsdp'=4,'ctx'=8,'tp'=4] {'ctx'}, dimensions={1}, use_global_device_ids=true | all-gather | bytes 36864 | tf_op jit(solution)/shard_map/all_gather | solution.py:216
  102.5 62.1 %all-gather.7.cloned.1.call-done = bf16[8,2048,3,64]{1,3,2,0:T(8,128)(2,1)} async-done(((bf16[8,256,3,64]{1,3,2,0:T(8,128)(2,1)}), bf16[8,2048,3,64]{1,3,2,0:T(8,128)(2,1)}) %all-gather.7.cloned.1.call-update) | async-done | bytes 6291472 | tf_op jit(solution)/shard_map/all_gather | solution.py:31
  164.5 12.8 %select_reduce_fusion = (f32[4,3,256]{2,1,0:T(4,128)S(1)}, f32[4,3,256,2048]{3,2,1,0:T(8,128)}) fusion(pred[4,256,2048]{2,1,0:T(8,128)(4,1)S(1)} %broadcast_compare_fusion.1, bf16[4,256,3,64]{1,3,2,0:T(8,128)(2,1)S(1)} %fusion.49, bf16[8,2048,3,64]{1,3,2,0:T(8,128)(2,1)} %all-gather.7.cloned.1.call-done), kind=kOutput, calls=%fused_computation.7 | convolution fusion | flops 824177664 | bytes 30814208 | tf_op jit(solution)/shard_map/sqhd,skhd->shqk/dot_general | solution.py:96
  177.3 12.0 %fusion = f32[4,3,256]{2,1,0:T(4,128)S(1)} fusion(f32[4,3,256,2048]{3,2,1,0:T(8,128)} %get-tuple-element.114, f32[4,3,256]{2,1,0:T(4,128)S(1)} %get-tuple-element.113, pred[4,256,2048]{2,1,0:T(8,128)(4,1)S(1)} %broadcast_compare_fusion.1), kind=kLoop, calls=%fused_computation.8 | loop fusion | flops 25162752 | bytes 27287552 | tf_op jit(solution)/shard_map/reduce_sum | solution.py:107
  189.3 13.3 %fusion.42 = bf16[4,256,3,64]{1,3,2,0:T(8,128)(2,1)S(1)} fusion(bf16[8,2048,3,64]{1,3,2,0:T(8,128)(2,1)} %all-gather.7.cloned.1.call-done, f32[4,3,256,2048]{3,2,1,0:T(8,128)} %get-tuple-element.114, f32[4,3,256]{2,1,0:T(4,128)S(1)} %fusion, f32[4,3,256]{2,1,0:T(4,128)S(1)} %get-tuple-element.113, pred[4,256,2048]{2,1,0:T(8,128)(4,1)S(1)} %broadcast_compare_fusion.1), kind=kOutput, calls=%fused_computation.90 | convolution fusion | flops 836960256 | bytes 33972224 | tf_op jit(solution)/shard_map/shqk,skhd->sqhd/dot_general | solution.py:109
  203.8 3.0 convolution_convert_fusion.3
  207.2 2.4 convert_reduce_fusion.1
  209.6 45.9 %all-reduce.7.cloned.1.call-done = bf16[1024,768]{1,0:T(8,128)(2,1)} async-done(((bf16[1024,768]{1,0:T(8,128)(2,1)}), bf16[1024,768]{1,0:T(8,128)(2,1)}) %all-reduce.7.cloned.1.call-update) | async-done | bytes 1572880 | tf_op jit(solution)/shard_map/psum | solution.py:221
  257.6 2.4 multiply_reduce_fusion.4
  260.1 9.6 %multiply_convert_fusion.4 = (bf16[1024,768]{1,0:T(8,128)(2,1)S(1)}, f32[1024,768]{1,0:T(8,128)}, f32[1024,768]{1,0:T(8,128)}) fusion(f32[768]{0:T(1024)S(1)} %convert_element_type.279, bf16[768,2310]{1,0:T(8,128)(2,1)S(1)} %copy-done.21, f32[1024,768]{1,0:T(8,128)S(1)} %get-tuple-element.93, f32[768]{0:T(1024)S(1)} %get-tuple-element.78, ...), kind=kOutput, calls=%fused_computation.49 | convolution fusion | flops 1263009792 | bytes 12206080 | tf_op jit(solution)/shard_map/dot_general | solution.py:225
  270.9 2.6 convolution_convert_fusion.2
  273.8 50.4 %all-reduce.9.cloned.1.call-done = bf16[1024,768]{1,0:T(8,128)(2,1)} async-done(((bf16[1024,768]{1,0:T(8,128)(2,1)}), bf16[1024,768]{1,0:T(8,128)(2,1)}) %all-reduce.9.cloned.1.call-update) | async-done | bytes 1572880 | tf_op jit(solution)/shard_map/psum | solution.py:230
  324.2 2.4 fusion.73
  329.8 2.6 fusion.72
  333.3 3.1 fusion.79
  337.6 2.6 convolution_convert_fusion
  340.3 50.6 %all-reduce.11.cloned.1.call-done = bf16[1024,768]{1,0:T(8,128)(2,1)} async-done(((bf16[1024,768]{1,0:T(8,128)(2,1)}), bf16[1024,768]{1,0:T(8,128)(2,1)}) %all-reduce.11.cloned.1.call-update) | async-done | bytes 1572880 | tf_op jit(solution)/shard_map/psum | solution.py:249
  390.9 4.4 multiply_reduce_fusion.1
  398.6 2.8 convolution_convert_fusion.7
  407.6 4.9 broadcast_compare_fusion
  413.2 4.2 convolution_convert_fusion.5
  417.4 2.6 reshape_reshape.3
  420.0 21.4 %multiply_reduce_fusion = (f32[4,3,256]{2,1,0:T(4,128)S(1)}, f32[4,3,256,2048]{3,2,1,0:T(8,128)}) fusion(f32[4,3,256,2048]{3,2,1,0:T(8,128)} %get-tuple-element.114, f32[4,3,256]{2,1,0:T(4,128)S(1)} %log_add_fusion, pred[4,256,2048]{2,1,0:T(8,128)(4,1)} %copy-done.1, bf16[8,2048,3,64]{1,3,2,0:T(8,128)(2,1)} %all-gather.7.cloned.1.call-done, ...), kind=kOutput, calls=%fused_computation.3 | convolution fusion | flops 836760576 | bytes 55992320 | tf_op jit(solution)/shard_map/sqhd,skhd->shqk/dot_general | solution.py:118
  441.5 19.5 %fusion.77 = (f32[3,64]{1,0:T(4,128)}, bf16[4,256,3,64]{1,3,2,0:T(8,128)(2,1)S(1)}) fusion(bf16[8,2048,3,64]{1,3,2,0:T(8,128)(2,1)S(1)} %bitcast.94, f32[4,3,256,2048]{3,2,1,0:T(8,128)} %get-tuple-element.117, f32[4,3,256,2048]{3,2,1,0:T(8,128)} %get-tuple-element.114, f32[4,3,256]{2,1,0:T(4,128)S(1)} %get-tuple-element.116, ...), kind=kOutput, calls=%fused_computation.166 | convolution fusion | flops 843644736 | bytes 59138816 | tf_op jit(solution)/shard_map/shqk,skhd->sqhd/dot_general | solution.py:123
  461.6 30.1 %all_gather.23 = f32[8,3,2048,1]{2,1,0,3:T(4,128)S(1)} all-gather(f32[8,3,256,1]{2,1,0,3:T(4,128)S(1)} %pad_maximum_fusion.2), channel_id=1, replica_groups=mesh['fsdp'=4,'ctx'=8,'tp'=4] {'ctx'}, dimensions={2}, use_global_device_ids=true | all-gather | bytes 221184 | tf_op jit(solution)/shard_map/all_gather | solution.py:31
  492.5 8.1 %all-gather.9.cloned.1.call-done = bf16[8,2048,3,64]{1,3,2,0:T(8,128)(2,1)} async-done(((bf16[8,256,3,64]{1,3,2,0:T(8,128)(2,1)}), bf16[8,2048,3,64]{1,3,2,0:T(8,128)(2,1)}) %all-gather.9.cloned.1.call-update) | async-done | bytes 6291472 | tf_op jit(solution)/shard_map/all_gather | solution.py:31
  500.6 12.3 %fusion.80 = f32[4,3,2048,256]{3,2,1,0:T(8,128)} fusion(bf16[8,2048,3,64]{1,3,2,0:T(8,128)(2,1)} %all-gather.9.cloned.1.call-done, bf16[4,256,3,64]{1,3,2,0:T(8,128)(2,1)S(1)} %copy-done.18), kind=kOutput, calls=%fused_computation.169 | convolution fusion | flops 805306368 | bytes 31850496 | tf_op jit(solution)/shard_map/sqhd,skhd->shqk/dot_general | solution.py:142
  512.9 10.1 %fusion.66 = f32[4,3,2048,256]{3,2,1,0:T(8,128)} fusion(bf16[8,2048,3,64]{1,3,2,0:T(8,128)(2,1)S(1)} %copy-done, bf16[4,256,3,64]{1,0,3,2:T(4,128)(2,1)S(1)} %copy-done.16), kind=kOutput, calls=%fused_computation.159 | convolution fusion | flops 805306368 | bytes 31850496 | tf_op jit(solution)/shard_map/sqhd,skhd->shqk/dot_general | solution.py:96
  523.0 16.5 %fusion.43 = bf16[4,256,3,64]{1,3,2,0:T(8,128)(2,1)S(1)} fusion(bf16[8,2048,3,64]{1,3,2,0:T(8,128)(2,1)S(1)} %copy-done, f32[4,3,2048,256]{3,2,1,0:T(8,128)} %fusion.80, f32[4,3,2048,256]{3,2,1,0:T(8,128)} %fusion.66, f32[4,3,2048]{2,1,0:T(4,128)S(1)} %get-tuple-element.106, f32[4,3,2048]{2,1,0:T(4,128)S(1)} %get-tuple-element.105, ...), kind=kOutput, calls=%fused_computation.91 | convolution fusion | flops 843448320 | bytes 59310080 | tf_op jit(solution)/shard_map/shqk,sqhd->skhd/dot_general | solution.py:146
  540.1 12.0 %fusion.78 = (f32[3,64]{1,0:T(4,128)}, bf16[4,256,3,64]{1,3,2,0:T(8,128)(2,1)S(1)}) fusion(bf16[8,2048,3,64]{1,3,2,0:T(8,128)(2,1)} %all-gather.9.cloned.1.call-done, f32[4,3,2048,256]{3,2,1,0:T(8,128)} %fusion.66, f32[4,3,2048]{2,1,0:T(4,128)S(1)} %get-tuple-element.105, pred[4,2048,256]{2,1,0:T(8,128)(4,1)S(1)} %copy-done.3), kind=kOutput, calls=%fused_computation.167 | convolution fusion | flops 830865216 | bytes 34046720 | tf_op jit(solution)/shard_map/shqk,sqhd->skhd/dot_general | solution.py:149
  554.3 4.3 bitcast_convert_fusion
  558.9 4.0 convolution_convert_fusion.4
  562.9 6.3 copy.144
  569.1 13.0 %reshape.337 = bf16[32,18432]{1,0:T(8,128)(2,1)} reshape(bf16[32,768,24]{2,1,0:T(8,128)(2,1)} %bitcast.95) | data formatting | bytes 2359296 | tf_op jit(solution)/shard_map/reshape | solution.py:56
  586.3 3.4 reshape.335
  591.3 3.8 fusion.33
  597.4 2.4 copy.141
  599.8 2.9 reshape.333
  606.0 2.5 constant_dynamic-update-slice_fusion.4
  609.5 21.0 %all-gather.11.cloned.1.call-done = bf16[1024,768]{1,0:T(8,128)(2,1)} async-done(((bf16[256,768]{1,0:T(8,128)(2,1)}), bf16[1024,768]{1,0:T(8,128)(2,1)}) %all-gather.11.cloned.1.call-update) | async-done | bytes 1572880 | tf_op jit(solution)/shard_map/all_gather | solution.py:43
  630.5 3.5 add_reduce_fusion
  643.0 4.1 pad.4
  647.1 5.2 reshape.338
  654.0 7.7 all-to-all-start
  662.9 6.3 all-to-all-done
  670.6 93.9 %all-reduce.13.cloned.1.call-done = bf16[14080,128]{1,0:T(8,128)(2,1)} async-done(((bf16[14080,128]{1,0:T(8,128)(2,1)}), bf16[14080,128]{1,0:T(8,128)(2,1)}) %all-reduce.13.cloned.1.call-update) | async-done | bytes 3604496
  (220 shorter events, 74.4 us)
Async XLA Ops:
  7.2 10.2 %copy-start.43 = (bf16[2,192]{1,0:T(2,128)(2,1)S(1)}, bf16[2,192]{1,0:T(2,128)(2,1)}, u32[]{:S(2)}) copy-start(bf16[2,192]{1,0:T(2,128)(2,1)} %param.18) | copy-start | bytes 2308
  7.2 56.6 %all-gather.5.cloned.1.call-start = ((), (), s32[]{:S(2)}) async-start(), calls=%async_computation.2 | async-start | bytes 4669440 | tf_op jit(solution)/shard_map/all_gather | solution.py:15
  14.1 51.7 %copy-start.10 = (bf16[4,256,768]{2,1,0:T(8,128)(2,1)S(1)}, bf16[4,256,768]{2,1,0:T(8,128)(2,1)}, u32[]{:S(2)}) copy-start(bf16[4,256,768]{2,1,0:T(8,128)(2,1)} %param.15) | copy-start | bytes 4718596
  17.3 147.2 %all-gather.7.cloned.1.call-start = ((), (), s32[]{:S(2)}) async-start(), calls=%async_computation.3 | async-start | bytes 7077888 | tf_op jit(solution)/shard_map/all_gather | solution.py:31
  65.7 2.2 copy-start.24
  67.9 2.8 copy-start.34
  70.6 184.9 %all-reduce.7.cloned.1.call-start = ((), (), s32[]{:S(2)}) async-start(), calls=%async_computation.4 | async-start | bytes 3145728 | tf_op jit(solution)/shard_map/psum | solution.py:221
  100.2 89.1 %copy-start.1 = (pred[4,256,2048]{2,1,0:T(8,128)(4,1)}, pred[4,256,2048]{2,1,0:T(8,128)(4,1)S(1)}, u32[]{:S(2)}) copy-start(pred[4,256,2048]{2,1,0:T(8,128)(4,1)S(1)} %broadcast_compare_fusion.1) | copy-start | bytes 6291460
  102.4 74.9 %copy-start.23 = (bf16[4,256,3,64]{1,3,2,0:T(8,128)(2,1)}, bf16[4,256,3,64]{1,3,2,0:T(8,128)(2,1)S(1)}, u32[]{:S(2)}) copy-start(bf16[4,256,3,64]{1,3,2,0:T(8,128)(2,1)S(1)} %fusion.49) | copy-start | bytes 1179652
  177.3 12.0 %copy-start.30 = (f32[4,3,256]{2,1,0:T(4,128)}, f32[4,3,256]{2,1,0:T(4,128)S(1)}, u32[]{:S(2)}) copy-start(f32[4,3,256]{2,1,0:T(4,128)S(1)} %get-tuple-element.113) | copy-start | bytes 36868
  189.3 13.4 %copy-start.31 = (f32[4,3,256]{2,1,0:T(4,128)}, f32[4,3,256]{2,1,0:T(4,128)S(1)}, u32[]{:S(2)}) copy-start(f32[4,3,256]{2,1,0:T(4,128)S(1)} %fusion) | copy-start | bytes 36868
  202.7 4.5 copy-start.41
  203.0 52.5 %copy-start.11 = (bf16[4,256,768]{2,1,0:T(8,128)(2,1)S(1)}, bf16[4,256,768]{2,1,0:T(8,128)(2,1)}, u32[]{:S(2)}) copy-start(bf16[4,256,768]{2,1,0:T(8,128)(2,1)} %param.15) | copy-start | bytes 4718596
  206.9 117.3 %all-reduce.9.cloned.1.call-start = ((), (), s32[]{:S(2)}) async-start(), calls=%async_computation.5 | async-start | bytes 3145728 | tf_op jit(solution)/shard_map/psum | solution.py:230
  209.6 114.6 %copy-start.36 = (f32[768]{0:T(1024)}, f32[768]{0:T(1024)S(1)}, u32[]{:S(2)}) copy-start(f32[768]{0:T(1024)S(1)} %get-tuple-element.78) | copy-start | bytes 9220
  209.6 185.7 %copy-start.26 = (f32[768]{0:T(1024)}, f32[768]{0:T(1024)S(1)}, u32[]{:S(2)}) copy-start(f32[768]{0:T(1024)S(1)} %get-tuple-element.79) | copy-start | bytes 9220
  257.6 2.5 copy-start.21
  260.1 135.2 %copy-start.27 = (f32[1024]{0:T(1024)}, f32[1024]{0:T(1024)S(1)}, u32[]{:S(2)}) copy-start(f32[1024]{0:T(1024)S(1)} %fusion.55) | copy-start | bytes 12292
  273.5 117.4 %all-reduce.11.cloned.1.call-start = ((), (), s32[]{:S(2)}) async-start(), calls=%async_computation.6 | async-start | bytes 3145728 | tf_op jit(solution)/shard_map/psum | solution.py:249
  328.0 4.5 copy-start.46
  329.8 2.7 copy-start.22
  329.8 3.5 copy-start.45
  332.4 4.0 copy-start.6
  332.4 62.9 %copy-start.32 = (f32[1024]{0:T(1024)}, f32[1024]{0:T(1024)S(1)}, u32[]{:S(2)}) copy-start(f32[1024]{0:T(1024)S(1)} %negate_multiply_fusion.2) | copy-start | bytes 12292
  340.2 160.3 %all-gather.9.cloned.1.call-start = ((), (), s32[]{:S(2)}) async-start(), calls=%async_computation.7 | async-start | bytes 7077888 | tf_op jit(solution)/shard_map/all_gather | solution.py:31
  390.9 4.4 copy-start.7
  390.9 4.4 copy-start.13
  404.7 200.9 %reduce-scatter.2.cloned.1.call-start = ((), (), s32[]{:S(2)}) async-start(), calls=%async_computation.8 | async-start | bytes 1966080 | tf_op jit(solution)/shard_map/reduce_scatter | solution.py:42
  417.4 24.1 %slice-start = ((s8[6291456]{0:T(1024)(128)(4,1)}), s8[2097152]{0:T(1024)(128)(4,1)S(1)}, s32[]{:S(2)}) async-start(s8[6291456]{0:T(1024)(128)(4,1)} %bitcast.93), calls=%async_computation.11 | async-start | bytes 4194304
  420.0 21.5 %slice-start.1 = ((s8[6291456]{0:T(1024)(128)(4,1)}), s8[4194304]{0:T(1024)(128)(4,1)S(1)}, s32[]{:S(2)}) async-start(s8[6291456]{0:T(1024)(128)(4,1)} %bitcast.93), calls=%async_computation.12 | async-start | bytes 8388608
  420.0 21.5 %copy-start.2 = (pred[4,256,2048]{2,1,0:T(8,128)(4,1)S(1)}, pred[4,256,2048]{2,1,0:T(8,128)(4,1)}, u32[]{:S(2)}) copy-start(pred[4,256,2048]{2,1,0:T(8,128)(4,1)} %copy-done.1) | copy-start | bytes 6291460
  461.0 39.6 %copy-start.18 = (bf16[4,256,3,64]{1,3,2,0:T(8,128)(2,1)S(1)}, bf16[4,256,3,64]{1,3,2,0:T(8,128)(2,1)}, u32[]{:S(2)}) copy-start(bf16[4,256,3,64]{1,3,2,0:T(8,128)(2,1)} %copy-done.17) | copy-start | bytes 1179652
  492.5 20.4 %copy-start.16 = (bf16[4,256,3,64]{1,0,3,2:T(4,128)(2,1)S(1)}, bf16[4,256,3,64]{1,0,3,2:T(4,128)(2,1)}, u32[]{:S(2)}) copy-start(bf16[4,256,3,64]{1,0,3,2:T(4,128)(2,1)} %copy-done.15) | copy-start | bytes 1179652
  500.6 12.3 %copy-start = (bf16[8,2048,3,64]{1,3,2,0:T(8,128)(2,1)S(1)}, bf16[8,2048,3,64]{1,3,2,0:T(8,128)(2,1)}, u32[]{:S(2)}) copy-start(bf16[8,2048,3,64]{1,3,2,0:T(8,128)(2,1)} %all-gather.9.cloned.1.call-done) | copy-start | bytes 18874372
  512.9 10.1 %copy-start.3 = (pred[4,2048,256]{2,1,0:T(8,128)(4,1)S(1)}, pred[4,2048,256]{2,1,0:T(8,128)(4,1)}, u32[]{:S(2)}) copy-start(pred[4,2048,256]{2,1,0:T(8,128)(4,1)} %broadcast_compare_fusion) | copy-start | bytes 6291460
  554.3 4.5 copy-start.8
  554.3 4.6 copy-start.33
  558.6 71.9 %all-gather.11.cloned.1.call-start = ((), (), s32[]{:S(2)}) async-start(), calls=%async_computation.9 | async-start | bytes 1966080 | tf_op jit(solution)/shard_map/all_gather | solution.py:43
  569.1 13.0 %copy-start.37 = (bf16[768]{0:T(1024)(128)(2,1)S(1)}, bf16[768]{0:T(1024)(128)(2,1)}, u32[]{:S(2)}) copy-start(bf16[768]{0:T(1024)(128)(2,1)} %get-tuple-element.72) | copy-start | bytes 4612
  569.1 13.1 %copy-start.5 = (f32[1024,768]{1,0:T(8,128)S(1)}, f32[1024,768]{1,0:T(8,128)}, u32[]{:S(2)}) copy-start(f32[1024,768]{1,0:T(8,128)} %copy-done.4) | copy-start | bytes 9437188
  569.1 13.1 %copy-start.20 = (bf16[24,8,4,256]{3,1,2,0:T(8,128)(2,1)S(1)}, bf16[24,8,4,256]{3,1,2,0:T(8,128)(2,1)}, u32[]{:S(2)}) copy-start(bf16[24,8,4,256]{3,1,2,0:T(8,128)(2,1)} %copy-done.19) | copy-start | bytes 1179652
  569.1 13.2 %copy-start.29 = (f32[1024]{0:T(1024)S(1)}, f32[1024]{0:T(1024)}, u32[]{:S(2)}) copy-start(f32[1024]{0:T(1024)} %copy-done.28) | copy-start | bytes 12292
  583.6 7.6 copy-start.38
  605.7 158.9 %all-reduce.13.cloned.1.call-start = ((), (), s32[]{:S(2)}) async-start(), calls=%async_computation.10 | async-start | bytes 7208960
  605.9 2.5 copy-start.14
  609.5 32.0 %copy-start.35 = (bf16[32,24]{1,0:T(8,128)(2,1)S(1)}, bf16[32,24]{1,0:T(8,128)(2,1)}, u32[]{:S(2)}) copy-start(bf16[32,24]{1,0:T(8,128)(2,1)} %convert_element_type.320) | copy-start | bytes 4612
  652.3 9.4 %copy-start.44 = (u32[128]{0:T(128)S(1)}, u32[128]{0:T(128)}, u32[]{:S(2)}) copy-start(u32[128]{0:T(128)} %constant.93) | copy-start | bytes 1540
  654.0 15.3 %all-to-all-start = ((f32[32,1,1152]{2,1,0:T(1,128)}), f32[32,1,1152]{2,1,0:T(1,128)S(1)}, u32[]{:S(2)}, u32[]{:S(2)}) async-start(f32[32,1,1152]{2,1,0:T(1,128)} %broadcast_in_dim.87), calls=%async_computation.1 | async-start | bytes 294912 | tf_op jit(solution)/shard_map/all_to_all | solution.py:69
  (13 other events, 16.6 us)
Sparse Core Ops, SparseCore 0:
  17.4 46.3 all-gather.4
  70.7 93.7 all-gather.6
  207.0 48.4 all-reduce.6
  273.6 50.4 all-reduce.8
  340.3 50.4 all-reduce.10
  404.8 95.7 all-gather.8
  558.7 22.8 reduce-scatter.1
  605.8 24.6 all-gather.10
  652.4 112.0 all-reduce.12
where the time goes:
time: 784 us; the launch traced here: 778 us
  waiting for transfers between devices  385 us (49%)
  matrix products  160 us (20%)
  local copies, waits for them, and re-layouts  99.4 us (13%)
  blocking collectives  58.2 us (7%)
  other arithmetic  50.8 us (6%)
  between operations  15.6 us (2%)
  starting transfers between devices  9.47 us (1%)
    unnamed x10, waiting for transfers between devices  94.1 us
    all_gather x2, waiting for transfers between devices, sent_together(): lax.all_gather(both, axis, axis=dim, tiled=True)  70.2 us
    psum x1, waiting for transfers between devices, shards(): lax.psum(norm_part.astype(jnp.bfloat16), 'tp').astype(jnp.float32)  50.6 us
    psum x1, waiting for transfers between devices, shards(): ffn_full = lax.psum(ffn_part.astype(jnp.bfloat16), 'tp').astype(jnp.float32)  50.4 us
    all_gather x1, waiting for transfers between devices, turned_gather(): out = lax.all_gather(both, axis, axis=0, tiled=True)  46.3 us
    psum x1, waiting for transfers between devices, shards(): lax.psum(attn_part.astype(jnp.bfloat16), 'tp').astype(jnp.float32)  45.9 us
    all_gather x1, blocking collectives, sent_together(): lax.all_gather(both, axis, axis=dim, tiled=True)  30.1 us
    all_gather x1, blocking collectives, shards(): lax.all_gather(segment_ids, 'ctx', axis=1, tiled=True)  28.1 us
  transfers between devices with their start and end apart: 10, of which 9 were waited for; matrix products, arithmetic and copies ran while one was open for 15% of the time, Pallas kernels for 0%

commit v1 on v0

--- a/solution.py
+++ b/solution.py
@@ -6,6 +6,11 @@
 HEAD_DIM = 64
 norm_eps = 1e-12
 masked_score = -1e30
+
+
+def all_by_exchange(x, mesh_axis, dim):
+    stack = jnp.stack([x] * lax.axis_size(mesh_axis))
+    return jnp.concatenate(lax.all_to_all(stack, mesh_axis, 0, 0), axis=dim)
 
 
 def turned_gather(arrays, axis, dims):
@@ -213,7 +218,7 @@
     value_rows = (proj_pre[2] + bias_pair[1]).astype(jnp.bfloat16).reshape(head_shape)
     all_keys, all_values, all_docs = (
         *sent_together((key_rows, value_rows), "ctx", 1, 0),
-        lax.all_gather(segment_ids, "ctx", axis=1, tiled=True),
+        all_by_exchange(segment_ids, "ctx", 1),
     )
     attended, log_total = whole_attention(queries, all_keys, all_values, segment_ids, all_docs)
     context = attended.reshape(row_count, local_cols).astype(jnp.bfloat16)

time: 784 us -> 815 us (1.040)
  waiting for transfers between devices: 385 us -> 411 us
    all_gather x1, waiting for transfers between devices: 21 us -> 34.6 us  [sum_by_parts(): whole = lax.all_gather(own, axis, axis=0, tiled=True)]
    unnamed x118 -> x116, local copies, waits for them, and re-layouts: 26.6 us -> 26.6 us
  transfers between devices with their start and end apart: 10 -> 11, of which waited for: 9 -> 9; matrix products, arithmetic and copies ran while one was open for 15% -> 14% of each run, Pallas kernels for 0% -> 0%
where the time goes in v1:
time: 815 us; the launch traced here: 810 us
  waiting for transfers between devices  411 us (50%)
  matrix products  160 us (20%)
  local copies, waits for them, and re-layouts  100 us (12%)
  blocking collectives  57.3 us (7%)
  other arithmetic  50 us (6%)
  between operations  15.6 us (2%)
  starting transfers between devices  15.5 us (2%)
    unnamed x10, waiting for transfers between devices  94.1 us
    all_gather x2, waiting for transfers between devices, sent_together(): lax.all_gather(both, axis, axis=dim, tiled=True)  76.7 us
    psum x1, waiting for transfers between devices, shards(): lax.psum(norm_part.astype(jnp.bfloat16), 'tp').astype(jnp.float32)  50.6 us
    psum x1, waiting for transfers between devices, shards(): ffn_full = lax.psum(ffn_part.astype(jnp.bfloat16), 'tp').astype(jnp.float32)  50.3 us
    all_gather x1, waiting for transfers between devices, turned_gather(): out = lax.all_gather(both, axis, axis=0, tiled=True)  46.3 us
    psum x1, waiting for transfers between devices, shards(): lax.psum(attn_part.astype(jnp.bfloat16), 'tp').astype(jnp.float32)  45.8 us
    all_gather x1, waiting for transfers between devices, sum_by_parts(): whole = lax.all_gather(own, axis, axis=0, tiled=True)  34.6 us
    all_gather x1, blocking collectives, shards(): lax.all_gather(segment_ids, 'ctx', axis=1, tiled=True)  28.7 us
  transfers between devices with their start and end apart: 11, of which 9 were waited for; matrix products, arithmetic and copies ran while one was open for 14% of the time, Pallas kernels for 0%

profile of v1, /device:TPU:1, one launch (start us, length us, event | category | flops | bytes accessed | tf_op | source)
XLA Modules:
  0.0 809.6 jit_solution(3039817415467251341)
XLA Ops:
  14.1 3.2 concatenate.18
  17.5 46.3 %all-gather.5.cloned.1.call-done = bf16[768,2310]{1,0:T(8,128)(2,1)} async-done(((bf16[192,2310]{1,0:T(8,128)(2,1)}), bf16[768,2310]{1,0:T(8,128)(2,1)}) %all-gather.5.cloned.1.call-update) | async-done | bytes 3548176 | tf_op jit(solution)/shard_map/all_gather | solution.py:20
  71.2 6.3 all-to-all-start
  77.8 6.3 all-to-all-done
  87.8 76.7 %all-gather.7.cloned.1.call-done = bf16[8,2048,3,64]{1,3,2,0:T(8,128)(2,1)} async-done(((bf16[8,256,3,64]{1,3,2,0:T(8,128)(2,1)}), bf16[8,2048,3,64]{1,3,2,0:T(8,128)(2,1)}) %all-gather.7.cloned.1.call-update) | async-done | bytes 6291472 | tf_op jit(solution)/shard_map/all_gather | solution.py:36
  164.4 12.8 %select_reduce_fusion = (f32[4,3,256]{2,1,0:T(4,128)S(1)}, f32[4,3,256,2048]{3,2,1,0:T(8,128)}) fusion(pred[4,256,2048]{2,1,0:T(8,128)(4,1)S(1)} %broadcast_compare_fusion.1, bf16[4,256,3,64]{1,3,2,0:T(8,128)(2,1)S(1)} %fusion.49, bf16[8,2048,3,64]{1,3,2,0:T(8,128)(2,1)} %all-gather.7.cloned.1.call-done), kind=kOutput, calls=%fused_computation.7 | convolution fusion | flops 824177664 | bytes 30814208 | tf_op jit(solution)/shard_map/sqhd,skhd->shqk/dot_general | solution.py:101
  177.2 12.0 %fusion = f32[4,3,256]{2,1,0:T(4,128)S(1)} fusion(f32[4,3,256,2048]{3,2,1,0:T(8,128)} %get-tuple-element.114, f32[4,3,256]{2,1,0:T(4,128)S(1)} %get-tuple-element.113, pred[4,256,2048]{2,1,0:T(8,128)(4,1)S(1)} %broadcast_compare_fusion.1), kind=kLoop, calls=%fused_computation.8 | loop fusion | flops 25162752 | bytes 27287552 | tf_op jit(solution)/shard_map/reduce_sum | solution.py:112
  189.2 13.3 %fusion.42 = bf16[4,256,3,64]{1,3,2,0:T(8,128)(2,1)S(1)} fusion(bf16[8,2048,3,64]{1,3,2,0:T(8,128)(2,1)} %all-gather.7.cloned.1.call-done, f32[4,3,256,2048]{3,2,1,0:T(8,128)} %get-tuple-element.114, f32[4,3,256]{2,1,0:T(4,128)S(1)} %fusion, f32[4,3,256]{2,1,0:T(4,128)S(1)} %get-tuple-element.113, pred[4,256,2048]{2,1,0:T(8,128)(4,1)S(1)} %broadcast_compare_fusion.1), kind=kOutput, calls=%fused_computation.90 | convolution fusion | flops 836960256 | bytes 33972224 | tf_op jit(solution)/shard_map/shqk,skhd->sqhd/dot_general | solution.py:114
  203.7 3.0 convolution_convert_fusion.3
  207.1 2.5 convert_reduce_fusion.1
  209.6 45.8 %all-reduce.7.cloned.1.call-done = bf16[1024,768]{1,0:T(8,128)(2,1)} async-done(((bf16[1024,768]{1,0:T(8,128)(2,1)}), bf16[1024,768]{1,0:T(8,128)(2,1)}) %all-reduce.7.cloned.1.call-update) | async-done | bytes 1572880 | tf_op jit(solution)/shard_map/psum | solution.py:226
  257.5 2.4 multiply_reduce_fusion.4
  260.0 9.6 %multiply_convert_fusion.4 = (bf16[1024,768]{1,0:T(8,128)(2,1)S(1)}, f32[1024,768]{1,0:T(8,128)}, f32[1024,768]{1,0:T(8,128)}) fusion(f32[768]{0:T(1024)S(1)} %convert_element_type.279, bf16[768,2310]{1,0:T(8,128)(2,1)S(1)} %copy-done.21, f32[1024,768]{1,0:T(8,128)S(1)} %get-tuple-element.93, f32[768]{0:T(1024)S(1)} %get-tuple-element.78, ...), kind=kOutput, calls=%fused_computation.49 | convolution fusion | flops 1263009792 | bytes 12206080 | tf_op jit(solution)/shard_map/dot_general | solution.py:230
  270.8 2.6 convolution_convert_fusion.2
  273.7 50.3 %all-reduce.9.cloned.1.call-done = bf16[1024,768]{1,0:T(8,128)(2,1)} async-done(((bf16[1024,768]{1,0:T(8,128)(2,1)}), bf16[1024,768]{1,0:T(8,128)(2,1)}) %all-reduce.9.cloned.1.call-update) | async-done | bytes 1572880 | tf_op jit(solution)/shard_map/psum | solution.py:235
  324.1 2.4 fusion.73
  329.7 2.6 fusion.72
  333.2 3.1 fusion.79
  337.5 2.6 convolution_convert_fusion
  340.2 50.6 %all-reduce.11.cloned.1.call-done = bf16[1024,768]{1,0:T(8,128)(2,1)} async-done(((bf16[1024,768]{1,0:T(8,128)(2,1)}), bf16[1024,768]{1,0:T(8,128)(2,1)}) %all-reduce.11.cloned.1.call-update) | async-done | bytes 1572880 | tf_op jit(solution)/shard_map/psum | solution.py:254
  390.8 4.4 multiply_reduce_fusion.1
  398.4 2.8 convolution_convert_fusion.7
  407.0 28.7 %all_gather.21 = s32[4,2048]{1,0:T(4,128)S(1)} all-gather(s32[4,256]{1,0:T(4,128)S(1)} %copy-done.29), channel_id=1, replica_groups=mesh['fsdp'=4,'ctx'=8,'tp'=4] {'ctx'}, dimensions={1}, use_global_device_ids=true | all-gather | bytes 36864 | tf_op jit(solution)/shard_map/all_gather | solution.py:271
  435.7 4.0 broadcast_compare_fusion
  440.5 4.1 convolution_convert_fusion.5
  444.6 2.6 reshape_reshape.3
  447.2 22.1 %multiply_reduce_fusion = (f32[4,3,256]{2,1,0:T(4,128)S(1)}, f32[4,3,256,2048]{3,2,1,0:T(8,128)}) fusion(f32[4,3,256,2048]{3,2,1,0:T(8,128)} %get-tuple-element.114, f32[4,3,256]{2,1,0:T(4,128)S(1)} %log_add_fusion, pred[4,256,2048]{2,1,0:T(8,128)(4,1)} %copy-done.1, bf16[8,2048,3,64]{1,3,2,0:T(8,128)(2,1)} %all-gather.7.cloned.1.call-done, ...), kind=kOutput, calls=%fused_computation.3 | convolution fusion | flops 836760576 | bytes 55992320 | tf_op jit(solution)/shard_map/sqhd,skhd->shqk/dot_general | solution.py:123
  469.3 18.7 %fusion.77 = (f32[3,64]{1,0:T(4,128)}, bf16[4,256,3,64]{1,3,2,0:T(8,128)(2,1)S(1)}) fusion(bf16[8,2048,3,64]{1,3,2,0:T(8,128)(2,1)S(1)} %bitcast.97, f32[4,3,256,2048]{3,2,1,0:T(8,128)} %get-tuple-element.117, f32[4,3,256,2048]{3,2,1,0:T(8,128)} %get-tuple-element.114, f32[4,3,256]{2,1,0:T(4,128)S(1)} %get-tuple-element.116, ...), kind=kOutput, calls=%fused_computation.166 | convolution fusion | flops 843644736 | bytes 59138816 | tf_op jit(solution)/shard_map/shqk,skhd->sqhd/dot_general | solution.py:128
  488.6 28.6 %all_gather.22 = f32[8,3,2048,1]{2,1,0,3:T(4,128)S(1)} all-gather(f32[8,3,256,1]{2,1,0,3:T(4,128)S(1)} %pad_maximum_fusion.2), channel_id=1, replica_groups=mesh['fsdp'=4,'ctx'=8,'tp'=4] {'ctx'}, dimensions={2}, use_global_device_ids=true | all-gather | bytes 221184 | tf_op jit(solution)/shard_map/all_gather | solution.py:36
  518.1 12.3 %fusion.80 = f32[4,3,2048,256]{3,2,1,0:T(8,128)} fusion(bf16[8,2048,3,64]{1,3,2,0:T(8,128)(2,1)} %all-gather.9.cloned.1.call-done, bf16[4,256,3,64]{1,3,2,0:T(8,128)(2,1)S(1)} %copy-done.18), kind=kOutput, calls=%fused_computation.169 | convolution fusion | flops 805306368 | bytes 31850496 | tf_op jit(solution)/shard_map/sqhd,skhd->shqk/dot_general | solution.py:147
  530.4 10.1 %fusion.66 = f32[4,3,2048,256]{3,2,1,0:T(8,128)} fusion(bf16[8,2048,3,64]{1,3,2,0:T(8,128)(2,1)S(1)} %copy-done, bf16[4,256,3,64]{1,0,3,2:T(4,128)(2,1)S(1)} %copy-done.16), kind=kOutput, calls=%fused_computation.159 | convolution fusion | flops 805306368 | bytes 31850496 | tf_op jit(solution)/shard_map/sqhd,skhd->shqk/dot_general | solution.py:101
  540.5 16.5 %fusion.43 = bf16[4,256,3,64]{1,3,2,0:T(8,128)(2,1)S(1)} fusion(bf16[8,2048,3,64]{1,3,2,0:T(8,128)(2,1)S(1)} %copy-done, f32[4,3,2048,256]{3,2,1,0:T(8,128)} %fusion.80, f32[4,3,2048,256]{3,2,1,0:T(8,128)} %fusion.66, f32[4,3,2048]{2,1,0:T(4,128)S(1)} %get-tuple-element.106, f32[4,3,2048]{2,1,0:T(4,128)S(1)} %get-tuple-element.105, ...), kind=kOutput, calls=%fused_computation.91 | convolution fusion | flops 843448320 | bytes 59310080 | tf_op jit(solution)/shard_map/shqk,sqhd->skhd/dot_general | solution.py:151
  557.6 12.0 %fusion.78 = (f32[3,64]{1,0:T(4,128)}, bf16[4,256,3,64]{1,3,2,0:T(8,128)(2,1)S(1)}) fusion(bf16[8,2048,3,64]{1,3,2,0:T(8,128)(2,1)} %all-gather.9.cloned.1.call-done, f32[4,3,2048,256]{3,2,1,0:T(8,128)} %fusion.66, f32[4,3,2048]{2,1,0:T(4,128)S(1)} %get-tuple-element.105, pred[4,2048,256]{2,1,0:T(8,128)(4,1)S(1)} %copy-done.3), kind=kOutput, calls=%fused_computation.167 | convolution fusion | flops 830865216 | bytes 34046720 | tf_op jit(solution)/shard_map/shqk,sqhd->skhd/dot_general | solution.py:154
  571.8 4.3 bitcast_convert_fusion
  576.4 4.0 convolution_convert_fusion.4
  580.4 6.3 copy.144
  586.7 13.0 %reshape.343 = bf16[32,18432]{1,0:T(8,128)(2,1)} reshape(bf16[32,768,24]{2,1,0:T(8,128)(2,1)} %bitcast.98) | data formatting | bytes 2359296 | tf_op jit(solution)/shard_map/reshape | solution.py:61
  603.9 3.4 reshape.341
  608.9 3.8 fusion.33
  617.5 2.9 reshape.339
  623.6 2.5 constant_dynamic-update-slice_fusion.4
  627.2 34.6 %all-gather.11.cloned.1.call-done = bf16[1024,768]{1,0:T(8,128)(2,1)} async-done(((bf16[256,768]{1,0:T(8,128)(2,1)}), bf16[1024,768]{1,0:T(8,128)(2,1)}) %all-gather.11.cloned.1.call-update) | async-done | bytes 1572880 | tf_op jit(solution)/shard_map/all_gather | solution.py:48
  661.8 3.5 add_reduce_fusion
  674.2 4.1 pad.4
  678.3 5.2 reshape.344
  685.2 7.7 all-to-all-start.1
  694.1 6.3 all-to-all-done.1
  701.8 94.0 %all-reduce.13.cloned.1.call-done = bf16[14080,128]{1,0:T(8,128)(2,1)} async-done(((bf16[14080,128]{1,0:T(8,128)(2,1)}), bf16[14080,128]{1,0:T(8,128)(2,1)}) %all-reduce.13.cloned.1.call-update) | async-done | bytes 3604496
  (221 shorter events, 77.1 us)
Async XLA Ops:
  7.2 10.2 %copy-start.42 = (bf16[2,192]{1,0:T(2,128)(2,1)S(1)}, bf16[2,192]{1,0:T(2,128)(2,1)}, u32[]{:S(2)}) copy-start(bf16[2,192]{1,0:T(2,128)(2,1)} %param.18) | copy-start | bytes 2308
  7.2 56.6 %all-gather.5.cloned.1.call-start = ((), (), s32[]{:S(2)}) async-start(), calls=%async_computation.3 | async-start | bytes 4669440 | tf_op jit(solution)/shard_map/all_gather | solution.py:20
  14.1 51.7 %copy-start.10 = (bf16[4,256,768]{2,1,0:T(8,128)(2,1)S(1)}, bf16[4,256,768]{2,1,0:T(8,128)(2,1)}, u32[]{:S(2)}) copy-start(bf16[4,256,768]{2,1,0:T(8,128)(2,1)} %param.15) | copy-start | bytes 4718596
  17.3 147.1 %all-gather.7.cloned.1.call-start = ((), (), s32[]{:S(2)}) async-start(), calls=%async_computation.4 | async-start | bytes 7077888 | tf_op jit(solution)/shard_map/all_gather | solution.py:36
  67.9 2.7 copy-start.29
  68.6 15.6 %copy-start.15 = (bf16[4,256,3,64]{1,0,3,2:T(4,128)(2,1)}, bf16[4,256,3,64]{1,0,3,2:T(4,128)(2,1)S(1)}, u32[]{:S(2)}) copy-start(bf16[4,256,3,64]{1,0,3,2:T(4,128)(2,1)S(1)} %convert_element_type.262) | copy-start | bytes 1179652
  71.2 12.9 %all-to-all-start = ((s32[8,4,256]{2,1,0:T(4,128)}), s32[8,4,256]{2,1,0:T(4,128)S(1)}, u32[]{:S(2)}, u32[]{:S(2)}) async-start(s32[8,4,256]{2,1,0:T(4,128)} %stack.11), calls=%async_computation | async-start | bytes 65536 | tf_op jit(solution)/shard_map/all_to_all | solution.py:13
  77.5 177.8 %all-reduce.7.cloned.1.call-start = ((), (), s32[]{:S(2)}) async-start(), calls=%async_computation.5 | async-start | bytes 3145728 | tf_op jit(solution)/shard_map/psum | solution.py:226
  85.5 103.7 %copy-start.1 = (pred[4,256,2048]{2,1,0:T(8,128)(4,1)}, pred[4,256,2048]{2,1,0:T(8,128)(4,1)S(1)}, u32[]{:S(2)}) copy-start(pred[4,256,2048]{2,1,0:T(8,128)(4,1)S(1)} %broadcast_compare_fusion.1) | copy-start | bytes 6291460
  87.8 89.5 %copy-start.23 = (bf16[4,256,3,64]{1,3,2,0:T(8,128)(2,1)}, bf16[4,256,3,64]{1,3,2,0:T(8,128)(2,1)S(1)}, u32[]{:S(2)}) copy-start(bf16[4,256,3,64]{1,3,2,0:T(8,128)(2,1)S(1)} %fusion.49) | copy-start | bytes 1179652
  177.2 12.0 %copy-start.30 = (f32[4,3,256]{2,1,0:T(4,128)}, f32[4,3,256]{2,1,0:T(4,128)S(1)}, u32[]{:S(2)}) copy-start(f32[4,3,256]{2,1,0:T(4,128)S(1)} %get-tuple-element.113) | copy-start | bytes 36868
  189.2 13.4 %copy-start.31 = (f32[4,3,256]{2,1,0:T(4,128)}, f32[4,3,256]{2,1,0:T(4,128)S(1)}, u32[]{:S(2)}) copy-start(f32[4,3,256]{2,1,0:T(4,128)S(1)} %fusion) | copy-start | bytes 36868
  202.6 4.4 copy-start.40
  202.9 52.5 %copy-start.11 = (bf16[4,256,768]{2,1,0:T(8,128)(2,1)S(1)}, bf16[4,256,768]{2,1,0:T(8,128)(2,1)}, u32[]{:S(2)}) copy-start(bf16[4,256,768]{2,1,0:T(8,128)(2,1)} %param.15) | copy-start | bytes 4718596
  206.8 117.3 %all-reduce.9.cloned.1.call-start = ((), (), s32[]{:S(2)}) async-start(), calls=%async_computation.6 | async-start | bytes 3145728 | tf_op jit(solution)/shard_map/psum | solution.py:235
  209.6 114.5 %copy-start.35 = (f32[768]{0:T(1024)}, f32[768]{0:T(1024)S(1)}, u32[]{:S(2)}) copy-start(f32[768]{0:T(1024)S(1)} %get-tuple-element.78) | copy-start | bytes 9220
  209.6 185.6 %copy-start.25 = (f32[768]{0:T(1024)}, f32[768]{0:T(1024)S(1)}, u32[]{:S(2)}) copy-start(f32[768]{0:T(1024)S(1)} %get-tuple-element.79) | copy-start | bytes 9220
  257.5 2.5 copy-start.21
  260.0 135.2 %copy-start.26 = (f32[1024]{0:T(1024)}, f32[1024]{0:T(1024)S(1)}, u32[]{:S(2)}) copy-start(f32[1024]{0:T(1024)S(1)} %fusion.55) | copy-start | bytes 12292
  273.4 117.3 %all-reduce.11.cloned.1.call-start = ((), (), s32[]{:S(2)}) async-start(), calls=%async_computation.7 | async-start | bytes 3145728 | tf_op jit(solution)/shard_map/psum | solution.py:254
  327.8 4.5 copy-start.45
  329.7 2.7 copy-start.22
  329.7 3.5 copy-start.44
  332.3 4.0 copy-start.6
  332.3 62.9 %copy-start.32 = (f32[1024]{0:T(1024)}, f32[1024]{0:T(1024)S(1)}, u32[]{:S(2)}) copy-start(f32[1024]{0:T(1024)S(1)} %negate_multiply_fusion.2) | copy-start | bytes 12292
  340.1 177.9 %all-gather.9.cloned.1.call-start = ((), (), s32[]{:S(2)}) async-start(), calls=%async_computation.8 | async-start | bytes 7077888 | tf_op jit(solution)/shard_map/all_gather | solution.py:36
  390.8 4.4 copy-start.7
  390.8 4.4 copy-start.13
  404.6 218.7 %reduce-scatter.2.cloned.1.call-start = ((), (), s32[]{:S(2)}) async-start(), calls=%async_computation.9 | async-start | bytes 1966080 | tf_op jit(solution)/shard_map/reduce_scatter | solution.py:47
  444.6 24.7 %slice-start = ((s8[6291456]{0:T(1024)(128)(4,1)}), s8[2097152]{0:T(1024)(128)(4,1)S(1)}, s32[]{:S(2)}) async-start(s8[6291456]{0:T(1024)(128)(4,1)} %bitcast.96), calls=%async_computation.12 | async-start | bytes 4194304
  447.2 22.1 %slice-start.1 = ((s8[6291456]{0:T(1024)(128)(4,1)}), s8[4194304]{0:T(1024)(128)(4,1)S(1)}, s32[]{:S(2)}) async-start(s8[6291456]{0:T(1024)(128)(4,1)} %bitcast.96), calls=%async_computation.13 | async-start | bytes 8388608
  447.2 22.1 %copy-start.2 = (pred[4,256,2048]{2,1,0:T(8,128)(4,1)S(1)}, pred[4,256,2048]{2,1,0:T(8,128)(4,1)}, u32[]{:S(2)}) copy-start(pred[4,256,2048]{2,1,0:T(8,128)(4,1)} %copy-done.1) | copy-start | bytes 6291460
  488.0 30.0 %copy-start.18 = (bf16[4,256,3,64]{1,3,2,0:T(8,128)(2,1)S(1)}, bf16[4,256,3,64]{1,3,2,0:T(8,128)(2,1)}, u32[]{:S(2)}) copy-start(bf16[4,256,3,64]{1,3,2,0:T(8,128)(2,1)} %copy-done.17) | copy-start | bytes 1179652
  518.0 12.4 %copy-start.16 = (bf16[4,256,3,64]{1,0,3,2:T(4,128)(2,1)S(1)}, bf16[4,256,3,64]{1,0,3,2:T(4,128)(2,1)}, u32[]{:S(2)}) copy-start(bf16[4,256,3,64]{1,0,3,2:T(4,128)(2,1)} %copy-done.15) | copy-start | bytes 1179652
  518.1 12.3 %copy-start = (bf16[8,2048,3,64]{1,3,2,0:T(8,128)(2,1)S(1)}, bf16[8,2048,3,64]{1,3,2,0:T(8,128)(2,1)}, u32[]{:S(2)}) copy-start(bf16[8,2048,3,64]{1,3,2,0:T(8,128)(2,1)} %all-gather.9.cloned.1.call-done) | copy-start | bytes 18874372
  530.4 10.1 %copy-start.3 = (pred[4,2048,256]{2,1,0:T(8,128)(4,1)S(1)}, pred[4,2048,256]{2,1,0:T(8,128)(4,1)}, u32[]{:S(2)}) copy-start(pred[4,2048,256]{2,1,0:T(8,128)(4,1)} %broadcast_compare_fusion) | copy-start | bytes 6291460
  571.8 4.6 copy-start.8
  571.8 4.6 copy-start.33
  576.1 85.7 %all-gather.11.cloned.1.call-start = ((), (), s32[]{:S(2)}) async-start(), calls=%async_computation.10 | async-start | bytes 1966080 | tf_op jit(solution)/shard_map/all_gather | solution.py:48
  586.7 13.1 %copy-start.36 = (bf16[768]{0:T(1024)(128)(2,1)S(1)}, bf16[768]{0:T(1024)(128)(2,1)}, u32[]{:S(2)}) copy-start(bf16[768]{0:T(1024)(128)(2,1)} %get-tuple-element.72) | copy-start | bytes 4612
  586.7 13.1 %copy-start.5 = (f32[1024,768]{1,0:T(8,128)S(1)}, f32[1024,768]{1,0:T(8,128)}, u32[]{:S(2)}) copy-start(f32[1024,768]{1,0:T(8,128)} %copy-done.4) | copy-start | bytes 9437188
  586.7 13.2 %copy-start.20 = (bf16[24,8,4,256]{3,1,2,0:T(8,128)(2,1)S(1)}, bf16[24,8,4,256]{3,1,2,0:T(8,128)(2,1)}, u32[]{:S(2)}) copy-start(bf16[24,8,4,256]{3,1,2,0:T(8,128)(2,1)} %copy-done.19) | copy-start | bytes 1179652
  586.7 13.2 %copy-start.28 = (f32[1024]{0:T(1024)S(1)}, f32[1024]{0:T(1024)}, u32[]{:S(2)}) copy-start(f32[1024]{0:T(1024)} %copy-done.27) | copy-start | bytes 12292
  601.2 7.6 copy-start.37
  623.3 172.5 %all-reduce.13.cloned.1.call-start = ((), (), s32[]{:S(2)}) async-start(), calls=%async_computation.11 | async-start | bytes 7208960
  627.2 45.5 %copy-start.34 = (bf16[32,24]{1,0:T(8,128)(2,1)S(1)}, bf16[32,24]{1,0:T(8,128)(2,1)}, u32[]{:S(2)}) copy-start(bf16[32,24]{1,0:T(8,128)(2,1)} %convert_element_type.320) | copy-start | bytes 4612
  683.5 9.4 %copy-start.43 = (u32[128]{0:T(128)S(1)}, u32[128]{0:T(128)}, u32[]{:S(2)}) copy-start(u32[128]{0:T(128)} %constant.93) | copy-start | bytes 1540
  685.2 15.3 %all-to-all-start.1 = ((f32[32,1,1152]{2,1,0:T(1,128)}), f32[32,1,1152]{2,1,0:T(1,128)S(1)}, u32[]{:S(2)}, u32[]{:S(2)}) async-start(f32[32,1,1152]{2,1,0:T(1,128)} %broadcast_in_dim.85), calls=%async_computation.2 | async-start | bytes 294912 | tf_op jit(solution)/shard_map/all_to_all | solution.py:74
  (13 other events, 17.8 us)
Sparse Core Ops, SparseCore 0:
  17.4 46.3 all-gather.4
  70.7 93.6 all-gather.6
  206.9 48.4 all-reduce.6
  273.5 50.4 all-reduce.8
  340.2 50.4 all-reduce.10
  404.7 93.7 all-gather.8
  576.2 36.5 reduce-scatter.1
  623.4 38.3 all-gather.10
  683.6 112.1 all-reduce.12
